TPU v7x, 512 devices: a whole 4x8x8 slice. The times are simulated.
512 devices in a mesh: wide: 64 (over x, y, core), narrow: 8 (over z).
Axes of the slice: x: 4, y: 8, z: 8, core: 2. Of those that a mesh axis runs over, the one named last changes fastest.
Arguments:
- points: bfloat16 [128, 1024, 512], P('wide', 'narrow'), may hold values from -6 to 6
- counts: int32 [128, 256], P('wide', 'narrow'), may hold values from 1 to 4, as said below
- destination: int32 [128, 256], P('wide', 'narrow'), may hold values from 0 to 63, as said below
- rotated_ball: int32 [128, 256], P('wide', 'narrow'), may hold values from 0 to 1
- qkv_first: bfloat16 [512, 1536], replicated, may hold values from -1 to 1
- out_first: bfloat16 [512, 512], replicated, may hold values from -0.25 to 0.25
- qkv_second: bfloat16 [512, 1536], replicated, may hold values from -1 to 1
- out_second: bfloat16 [512, 512], replicated, may hold values from -0.25 to 0.25
Outputs:
- result: bfloat16 [128, 1024, 512], P('wide', 'narrow')
Inputs may be any that keep to these rules, and one draw needn't show every extreme that they name: `counts`: the first block of every ball row has all 4 points usable. Among the blocks of one device, at most 2 have the same destination; on every device some destination receives 2 of its blocks, and some destination receives 2 blocks from every device of its narrow index.
All inputs are finite; a program needn't handle non-finite values.
Results may differ from a plain program's by a relative error of at most 0.0095.
Values may be sent and summed in bfloat16 or wider, within the bound.
A program may use at most 64 MiB of HBM per device.

v0:
```python
import math
import jax
import jax.numpy as jnp
from jax import lax
from jax.sharding import PartitionSpec as P

HEADS = 8
BLK = 4
EPSILON = 1e-06
NEGATIVE = -1e30


def rms_round(values):
    widened = values.astype(jnp.float32)
    scaled = widened * lax.rsqrt(jnp.mean(widened * widened, axis=-1, keepdims=True) + EPSILON)
    return scaled.astype(jnp.bfloat16)


def project(normed, weight):
    flat = normed.reshape(-1, normed.shape[-1])
    product = jnp.dot(flat, weight, preferred_element_type=jnp.float32)
    return product.reshape(normed.shape[:-1] + (weight.shape[1],))


def split_heads(block_rows, offset, model_width):
    head_dim = model_width // HEADS
    return block_rows[..., offset : offset + model_width].reshape(
        block_rows.shape[:-1] + (HEADS, head_dim)
    )


def usable_points(counts):
    position = lax.broadcasted_iota(jnp.int32, counts.shape + (BLK,), len(counts.shape))
    usable = position < counts[..., None]
    return usable.reshape(counts.shape[:-1] + (counts.shape[-1] * BLK,))


def pool_rows(qkv_all, counts):
    model_width = qkv_all.shape[-1] // 3
    usable = usable_points(counts)
    kv_part = qkv_all[..., model_width:].astype(jnp.float32) * usable[..., None].astype(jnp.float32)
    grouped = kv_part.reshape(counts.shape + (BLK, 2 * model_width)).sum(axis=-2)
    return (grouped / counts[..., None].astype(jnp.float32)).astype(jnp.bfloat16)


def fine_coarse(ball_qkv, fine_usable, coarse_kv):
    model_width = coarse_kv.shape[-1] // 2
    scaling = 1.0 / math.sqrt(model_width // HEADS)
    queries = split_heads(ball_qkv, 0, model_width)
    key_fine = split_heads(ball_qkv, model_width, model_width)
    value_fine = split_heads(ball_qkv, 2 * model_width, model_width)
    key_coarse = split_heads(coarse_kv, 0, model_width)
    value_coarse = split_heads(coarse_kv, model_width, model_width)
    score_fine = (
        jnp.einsum("qhe,khe->hqk", queries, key_fine, preferred_element_type=jnp.float32) * scaling
    )
    score_fine = jnp.where(fine_usable[None, None, :], score_fine, NEGATIVE)
    score_coarse = (
        jnp.einsum("qhe,khe->hqk", queries, key_coarse, preferred_element_type=jnp.float32)
        * scaling
    )
    highest = jnp.maximum(jnp.max(score_fine, axis=-1), jnp.max(score_coarse, axis=-1))[..., None]
    exp_fine = jnp.exp(score_fine - highest)
    exp_coarse = jnp.exp(score_coarse - highest)
    denominator = jnp.sum(exp_fine, axis=-1, keepdims=True) + jnp.sum(
        exp_coarse, axis=-1, keepdims=True
    )
    weight_fine = (exp_fine / denominator).astype(jnp.bfloat16)
    weight_coarse = (exp_coarse / denominator).astype(jnp.bfloat16)
    mixture = jnp.einsum(
        "hqk,khe->qhe", weight_fine, value_fine, preferred_element_type=jnp.float32
    )
    mixture = mixture + jnp.einsum(
        "hqk,khe->qhe", weight_coarse, value_coarse, preferred_element_type=jnp.float32
    )
    return mixture.reshape(mixture.shape[0], model_width).astype(jnp.bfloat16)


def ball_attention(recv_rows, row_ball, row_usable):
    total_rows = recv_rows.shape[0]
    model_width = recv_rows.shape[1] // 3
    scaling = 1.0 / math.sqrt(model_width // HEADS)
    queries = split_heads(recv_rows, 0, model_width)
    key_rows = split_heads(recv_rows, model_width, model_width)
    value_rows = split_heads(recv_rows, 2 * model_width, model_width)
    block_len = min(256, total_rows)

    def one_block(block_idx):
        offset = block_idx * block_len
        query_block = lax.dynamic_slice_in_dim(queries, offset, block_len, 0)
        ball_block = lax.dynamic_slice_in_dim(row_ball, offset, block_len, 0)
        scores = (
            jnp.einsum("qhe,khe->hqk", query_block, key_rows, preferred_element_type=jnp.float32)
            * scaling
        )
        allowed = (ball_block[:, None] == row_ball[None, :]) & row_usable[None, :]
        scores = jnp.where(allowed[None], scores, NEGATIVE)
        highest = jnp.max(scores, axis=-1, keepdims=True)
        exponent = jnp.exp(scores - highest)
        weights = (exponent / jnp.sum(exponent, axis=-1, keepdims=True)).astype(jnp.bfloat16)
        mixture = jnp.einsum(
            "hqk,khe->qhe", weights, value_rows, preferred_element_type=jnp.float32
        )
        return mixture.reshape(block_len, model_width).astype(jnp.bfloat16)

    blocks_out = lax.map(one_block, jnp.arange(total_rows // block_len, dtype=jnp.int32))
    return blocks_out.reshape(total_rows, model_width)


def on_device(
    points, counts, destination, rotated_ball, qkv_first, out_first, qkv_second, out_second
):
    model_width = points.shape[-1]
    normed_one = rms_round(points)
    qkv_one = project(normed_one, qkv_first).astype(jnp.bfloat16)
    pooled = pool_rows(qkv_one, counts)
    usable = usable_points(counts)
    pooled_all = lax.all_gather(pooled, "narrow", axis=1, tiled=True)
    attended_one = jax.vmap(fine_coarse)(qkv_one, usable, pooled_all)
    layer_one = (points.astype(jnp.float32) + project(attended_one, out_first)).astype(jnp.bfloat16)
    normed_two = rms_round(layer_one)
    wide_count = lax.axis_size("wide")
    block_count = destination.size
    capacity = max(2, 2 * block_count // wide_count)
    dest_flat = destination.reshape(block_count)
    ball_flat = rotated_ball.reshape(block_count)
    fill_flat = counts.reshape(block_count)
    onehot = (dest_flat[:, None] == jnp.arange(wide_count, dtype=jnp.int32)[None, :]).astype(
        jnp.int32
    )
    earlier = jnp.cumsum(onehot, axis=0, dtype=jnp.int32) - onehot
    rank_in = jnp.sum(earlier * onehot, axis=1, dtype=jnp.int32)
    slot_of = dest_flat * capacity + rank_in

    def packed(block_data, filler):
        buffer = jnp.full((wide_count * capacity,) + block_data.shape[1:], filler, block_data.dtype)
        return (
            buffer.at[slot_of]
            .set(block_data)
            .reshape((wide_count, capacity) + block_data.shape[1:])
        )

    ball_packed = packed(ball_flat, -1)
    fill_packed = packed(fill_flat, 0)
    qkv_two = project(normed_two, qkv_second).astype(jnp.bfloat16)
    qkv_blocks = qkv_two.reshape(block_count, BLK, 3 * model_width)
    arrived, ball_in, fill_in = (
        lax.all_to_all(packed(qkv_blocks, 0), "wide", split_axis=0, concat_axis=0, tiled=True),
        lax.all_to_all(ball_packed, "wide", split_axis=0, concat_axis=0, tiled=True),
        lax.all_to_all(fill_packed, "wide", split_axis=0, concat_axis=0, tiled=True),
    )
    recv_rows = arrived.reshape(-1, 3 * model_width)
    row_ball = jnp.broadcast_to(ball_in[..., None], ball_in.shape + (BLK,)).reshape(-1)
    row_usable = usable_points(fill_in).reshape(-1)
    mixture = ball_attention(recv_rows, row_ball, row_usable)
    returned = lax.all_to_all(
        mixture.reshape(wide_count, capacity, BLK, model_width),
        "wide",
        split_axis=0,
        concat_axis=0,
        tiled=True,
    )
    attended_two = returned.reshape(wide_count * capacity, BLK, model_width)[slot_of].reshape(
        points.shape
    )
    return (layer_one.astype(jnp.float32) + project(attended_two, out_second)).astype(jnp.bfloat16)


def solution(mesh):
    in_specs = (
        P("wide", "narrow", None),
        P("wide", "narrow"),
        P("wide", "narrow"),
        P("wide", "narrow"),
        P(),
        P(),
        P(),
        P(),
    )
    out_specs = P("wide", "narrow", None)
    return jax.shard_map(
        on_device, mesh=mesh, in_specs=in_specs, out_specs=out_specs, check_vma=False
    )
```

profile of v0, /device:TPU:1, one launch (start us, length us, event | category | flops | bytes accessed | tf_op | source)
XLA Modules:
  0.0 210.0 jit_solution(17064649044195788203)
XLA Ops:
  9.4 1.6 convolution_convert_fusion.1
  12.1 1.6 reshape.243
  13.7 1.4 reduce_sum.66
  19.1 11.6 %all-to-all-start = ((s32[64,1,2]{2,1,0:T(1,128)}), s32[64,1,2]{2,1,0:T(1,128)S(1)}, u32[]{:S(2)}, u32[]{:S(2)}) async-start(s32[64,1,2]{2,1,0:T(1,128)} %bitcast.11), calls=%async_computation | async-start | bytes 65536 | tf_op jit(solution)/shard_map/all_to_all | solution.py:149
  32.3 27.9 %all-gather.2.cloned.1.call-done = bf16[2,256,1024]{2,0,1:T(2,128)(2,1)} async-done(((bf16[2,32,1024]{2,0,1:T(2,128)(2,1)}), bf16[2,256,1024]{2,0,1:T(2,128)(2,1)}) %all-gather.2.cloned.1.call-update) | async-done | bytes 1048592 | tf_op jit(solution)/shard_map/all_gather | solution.py:118
  60.2 2.7 %fusion.57 = (bf16[2,256,512]{2,0,1:T(2,128)(2,1)S(1)}, bf16[2,256,512]{2,0,1:T(2,128)(2,1)}) fusion(bf16[2,256,1024]{2,0,1:T(2,128)(2,1)} %all-gather.2.cloned.1.call-done), kind=kLoop, calls=%fused_computation.79 | loop fusion | bytes 2097152 | tf_op jit(solution)/shard_map/vmap()/slice | solution.py:27
  63.0 2.0 copy.52
  65.0 1.6 multiply_reduce_fusion
  74.9 1.6 broadcast_in_dim.71
  76.4 8.1 %scatter_fusion = bf16[128,4,1536]{2,1,0:T(4,128)(2,1)} fusion(bf16[128,4,1536]{2,1,0:T(4,128)(2,1)} %broadcast_in_dim.71, s32[64]{0:T(128)S(1)} %fusion.44, bf16[64,4,1536]{2,1,0:T(4,128)(2,1)S(1)} %reshape.284), kind=kCustom, calls=%fused_computation.3 | custom fusion | bytes 2359552 | tf_op jit(solution)/shard_map/scatter | solution.py:139
  84.5 15.0 %all-to-all-start.2 = ((bf16[64,2,4,1536]{3,2,1,0:T(4,128)(2,1)}), bf16[64,2,4,1536]{3,2,1,0:T(4,128)(2,1)S(1)}, u32[]{:S(2)}, u32[]{:S(2)}) async-start(bf16[64,2,4,1536]{3,2,1,0:T(4,128)(2,1)} %bitcast.14), calls=%async_computation.2 | async-start | bytes 3145728 | tf_op jit(solution)/shard_map/all_to_all | solution.py:148
  101.6 37.7 %all-to-all-done.2 = bf16[64,2,4,1536]{3,2,1,0:T(4,128)(2,1)S(1)} async-done(((bf16[64,2,4,1536]{3,2,1,0:T(4,128)(2,1)}), bf16[64,2,4,1536]{3,2,1,0:T(4,128)(2,1)S(1)}, u32[]{:S(2)}, u32[]{:S(2)}) %all-to-all-start.2) | async-done | bytes 1572896 | tf_op jit(solution)/shard_map/all_to_all | solution.py:148
  139.3 6.1 %all-to-all-start.1 = ((s32[64,1,2]{2,1,0:T(1,128)}), s32[64,1,2]{2,1,0:T(1,128)S(1)}, u32[]{:S(2)}, u32[]{:S(2)}) async-start(s32[64,1,2]{2,1,0:T(1,128)} %bitcast.18), calls=%async_computation.1 | async-start | bytes 65536 | tf_op jit(solution)/shard_map/all_to_all | solution.py:150
  145.5 1.4 reshape.251
  146.8 1.5 fusion.56
  150.5 4.1 %all-to-all-done.1 = s32[64,1,2]{2,1,0:T(1,128)S(1)} async-done(((s32[64,1,2]{2,1,0:T(1,128)}), s32[64,1,2]{2,1,0:T(1,128)S(1)}, u32[]{:S(2)}, u32[]{:S(2)}) %all-to-all-start.1) | async-done | bytes 544 | tf_op jit(solution)/shard_map/all_to_all | solution.py:150
  154.7 20.9 %while.11 = (s32[]{:T(128)}, bf16[2,256,512]{2,1,0:T(8,128)(2,1)}, s32[2]{0:T(128)S(1)}, s32[512]{0:T(512)S(1)}, bf16[512,8,64]{0,2,1:T(8,128)(2,1)S(1)}, /*inde...) while((s32[]{:T(128)}, bf16[2,256,512]{2,1,0:T(8,128)(2,1)}, ...), condition=%wide.region_15.16_spmd.clone, body=%wide.region_12.15_spmd.clone.sunk | while | flops 275121152 | bytes 11303615 | solution.py:106
  156.7 4.5 %fusion.79 = (f32[8,256]{1,0:T(8,128)S(1)}, f32[8,256,512]{2,1,0:T(8,128)}) fusion(pred[256,512]{1,0:T(8,128)(4,1)S(1)} %compare_and_fusion.2, bf16[512,8,64]{0,2,1:T(8,128)(2,1)} %get-tuple-element.229, bf16[512,8,64]{0,2,1:T(8,128)(2,1)S(1)} %get-tuple-element.228, s32[]{:T(128)S(6)} %select_n.46), kind=kOutput, calls=%fused_computation.77.clone.1 | convolution fusion | flops 138412544 | bytes 5120004 | tf_op jit(solution)/shard_map/while/body/eval_jaxpr/sub | solution.py:99
  161.2 3.0 %fusion.80 = bf16[8,256,64]{1,2,0:T(8,128)(2,1)S(1)} fusion(bf16[512,8,64]{0,2,1:T(8,128)(2,1)S(1)} %get-tuple-element.230, f32[8,256,512]{2,1,0:T(8,128)} %get-tuple-element.196, f32[8,256]{1,0:T(8,128)S(1)} %get-tuple-element.197), kind=kOutput, calls=%fused_computation.15.clone.1 | convolution fusion | flops 136445952 | bytes 4988928 | tf_op jit(solution)/shard_map/while/body/eval_jaxpr/hqk,khe->qhe/dot_general | solution.py:101
  167.1 4.5 %fusion.79 = (f32[8,256]{1,0:T(8,128)S(1)}, f32[8,256,512]{2,1,0:T(8,128)}) fusion(pred[256,512]{1,0:T(8,128)(4,1)S(1)} %compare_and_fusion.2, bf16[512,8,64]{0,2,1:T(8,128)(2,1)} %get-tuple-element.229, bf16[512,8,64]{0,2,1:T(8,128)(2,1)S(1)} %get-tuple-element.228, s32[]{:T(128)S(6)} %select_n.46), kind=kOutput, calls=%fused_computation.77.clone.1 | convolution fusion | flops 138412544 | bytes 5120004 | tf_op jit(solution)/shard_map/while/body/eval_jaxpr/sub | solution.py:99
  171.7 3.0 %fusion.80 = bf16[8,256,64]{1,2,0:T(8,128)(2,1)S(1)} fusion(bf16[512,8,64]{0,2,1:T(8,128)(2,1)S(1)} %get-tuple-element.230, f32[8,256,512]{2,1,0:T(8,128)} %get-tuple-element.196, f32[8,256]{1,0:T(8,128)S(1)} %get-tuple-element.197), kind=kOutput, calls=%fused_computation.15.clone.1 | convolution fusion | flops 136445952 | bytes 4988928 | tf_op jit(solution)/shard_map/while/body/eval_jaxpr/hqk,khe->qhe/dot_general | solution.py:101
  175.6 2.1 reshape_reshape.4
  177.7 6.2 %all-to-all-start.3 = ((bf16[64,2,4,512]{3,2,1,0:T(4,128)(2,1)}), bf16[64,2,4,512]{3,2,1,0:T(4,128)(2,1)S(1)}, u32[]{:S(2)}, u32[]{:S(2)}) async-start(bf16[64,2,4,512]{3,2,1,0:T(4,128)(2,1)} %reshape_reshape.4), calls=%async_computation.3 | async-start | bytes 1048576 | tf_op jit(solution)/shard_map/all_to_all | solution.py:156
  183.9 17.3 %all-to-all-done.3 = bf16[64,2,4,512]{3,2,1,0:T(4,128)(2,1)S(1)} async-done(((bf16[64,2,4,512]{3,2,1,0:T(4,128)(2,1)}), bf16[64,2,4,512]{3,2,1,0:T(4,128)(2,1)S(1)}, u32[]{:S(2)}, u32[]{:S(2)}) %all-to-all-start.3) | async-done | bytes 524320 | tf_op jit(solution)/shard_map/all_to_all | solution.py:156
  (104 shorter events, 28.4 us)
Async XLA Ops:
  6.5 2.9 %copy-start = (bf16[512,1536]{1,0:T(8,128)(2,1)S(1)}, bf16[512,1536]{1,0:T(8,128)(2,1)}, u32[]{:S(2)}) copy-start(bf16[512,1536]{1,0:T(8,128)(2,1)} %param.14) | copy-start | bytes 4718596
  6.5 53.7 %all-gather.2.cloned.1.call-start = ((), (), s32[]{:S(2)}) async-start(), calls=%async_computation.4 | async-start | bytes 1179648 | tf_op jit(solution)/shard_map/all_gather | solution.py:118
  12.1 4.8 %copy-start.13 = (s32[2,32]{1,0:T(2,128)S(1)}, s32[2,32]{1,0:T(2,128)}, u32[]{:S(2)}) copy-start(s32[2,32]{1,0:T(2,128)} %param.12) | copy-start | bytes 772
  12.1 5.0 %copy-start.14 = (s32[2,32]{1,0:T(2,128)S(1)}, s32[2,32]{1,0:T(2,128)}, u32[]{:S(2)}) copy-start(s32[2,32]{1,0:T(2,128)} %param.13) | copy-start | bytes 772
  19.1 65.5 %all-to-all-start = ((s32[64,1,2]{2,1,0:T(1,128)}), s32[64,1,2]{2,1,0:T(1,128)S(1)}, u32[]{:S(2)}, u32[]{:S(2)}) async-start(s32[64,1,2]{2,1,0:T(1,128)} %bitcast.11), calls=%async_computation | async-start | bytes 65536 | tf_op jit(solution)/shard_map/all_to_all | solution.py:149
  66.6 1.4 copy-start.1
  66.6 3.3 %copy-start.11 = (bf16[2,128,512]{1,2,0:T(8,128)(2,1)S(1)}, bf16[2,128,512]{1,2,0:T(8,128)(2,1)}, u32[]{:S(2)}) copy-start(bf16[2,128,512]{1,2,0:T(8,128)(2,1)} %copy.48) | copy-start | bytes 786436
  69.9 1.6 copy-start.2
  69.9 1.7 copy-start.9
  71.6 1.1 copy-start.5
  71.6 1.1 copy-start.10
  72.7 1.4 copy-start.6
  73.1 0.8 copy-start.3
  84.5 15.0 %copy-start.12 = (s32[2,32]{1,0:T(2,128)S(1)}, s32[2,32]{1,0:T(2,128)}, u32[]{:S(2)}) copy-start(s32[2,32]{1,0:T(2,128)} %param.11) | copy-start | bytes 772
  84.5 54.8 %all-to-all-start.2 = ((bf16[64,2,4,1536]{3,2,1,0:T(4,128)(2,1)}), bf16[64,2,4,1536]{3,2,1,0:T(4,128)(2,1)S(1)}, u32[]{:S(2)}, u32[]{:S(2)}) async-start(bf16[64,2,4,1536]{3,2,1,0:T(4,128)(2,1)} %bitcast.14), calls=%async_computation.2 | async-start | bytes 3145728 | tf_op jit(solution)/shard_map/all_to_all | solution.py:148
  139.3 15.3 %all-to-all-start.1 = ((s32[64,1,2]{2,1,0:T(1,128)}), s32[64,1,2]{2,1,0:T(1,128)S(1)}, u32[]{:S(2)}, u32[]{:S(2)}) async-start(s32[64,1,2]{2,1,0:T(1,128)} %bitcast.18), calls=%async_computation.1 | async-start | bytes 65536 | tf_op jit(solution)/shard_map/all_to_all | solution.py:150
  149.3 5.4 %copy-start.8 = (bf16[512,512]{0,1:T(8,128)(2,1)S(1)}, bf16[512,512]{0,1:T(8,128)(2,1)}, u32[]{:S(2)}) copy-start(bf16[512,512]{0,1:T(8,128)(2,1)} %copy.59) | copy-start | bytes 1572868
  175.6 26.5 %copy-start.4 = (f32[2,128,512]{2,1,0:T(8,128)S(1)}, f32[2,128,512]{2,1,0:T(8,128)}, u32[]{:S(2)}) copy-start(f32[2,128,512]{2,1,0:T(8,128)} %copy-done.3) | copy-start | bytes 1572868
  175.6 26.5 %copy-start.7 = (bf16[512,512]{1,0:T(8,128)(2,1)S(1)}, bf16[512,512]{1,0:T(8,128)(2,1)}, u32[]{:S(2)}) copy-start(bf16[512,512]{1,0:T(8,128)(2,1)} %param.17) | copy-start | bytes 1572868
  177.7 23.5 %all-to-all-start.3 = ((bf16[64,2,4,512]{3,2,1,0:T(4,128)(2,1)}), bf16[64,2,4,512]{3,2,1,0:T(4,128)(2,1)S(1)}, u32[]{:S(2)}, u32[]{:S(2)}) async-start(bf16[64,2,4,512]{3,2,1,0:T(4,128)(2,1)} %reshape_reshape.4), calls=%async_computation.3 | async-start | bytes 1048576 | tf_op jit(solution)/shard_map/all_to_all | solution.py:156
Sparse Core Ops, SparseCore 0:
  17.0 43.1 all-gather.1
where the time goes:
time: 211 us; the launch traced here: 210 us
  waiting for transfers between devices  87.1 us (41%)
  local copies, waits for them, and re-layouts  39.5 us (19%)
  starting transfers between devices  39 us (18%)
  matrix products  22 us (10%)
  between operations  13.7 us (6%)
  other arithmetic  7.28 us (3%)
    all_to_all x1, waiting for transfers between devices, on_device(): lax.all_to_all(packed(qkv_blocks, 0), 'wide', split_axis=0, concat_axis=0...  37.7 us
    all_gather x1, waiting for transfers between devices, on_device(): pooled_all = lax.all_gather(pooled, 'narrow', axis=1, tiled=True)  27.9 us
    all_to_all x1, waiting for transfers between devices, on_device(): lax.all_to_all(mixture.reshape(wide_count, capacity, BLK, model_width), '...  17.3 us
    all_to_all x1, starting transfers between devices, on_device(): lax.all_to_all(packed(qkv_blocks, 0), 'wide', split_axis=0, concat_axis=0...  15 us
    all_to_all x1, starting transfers between devices, on_device(): lax.all_to_all(ball_packed, 'wide', split_axis=0, concat_axis=0, tiled=True)  11.6 us
    slice x11, local copies, waits for them, and re-layouts, split_heads(): block_rows[..., offset:offset + model_width]  10.9 us
    scatter x3, local copies, waits for them, and re-layouts, packed(): return buffer.at[slot_of].set(block_data).reshape((wide_count, capacity)...  9.62 us
    sub x2, matrix products, one_block(): exponent = jnp.exp(scores - highest)  9.07 us
  transfers between devices with their start and end apart: 5, of which 4 were waited for; matrix products, arithmetic and copies ran while one was open for 14% of the time, Pallas kernels for 0%

commit v1 on v0

--- a/solution.py
+++ b/solution.py
@@ -3,6 +3,7 @@
 import jax.numpy as jnp
 from jax import lax
 from jax.sharding import PartitionSpec as P
+from jax.lax import all_to_all, psum
 
 HEADS = 8
 BLK = 4
@@ -115,7 +116,9 @@
     qkv_one = project(normed_one, qkv_first).astype(jnp.bfloat16)
     pooled = pool_rows(qkv_one, counts)
     usable = usable_points(counts)
-    pooled_all = lax.all_gather(pooled, "narrow", axis=1, tiled=True)
+    pooled_all = jnp.concatenate(
+        all_to_all(jnp.stack([pooled] * psum(1, "narrow"), 0), "narrow", 0, 0), axis=1
+    )
     attended_one = jax.vmap(fine_coarse)(qkv_one, usable, pooled_all)
     layer_one = (points.astype(jnp.float32) + project(attended_one, out_first)).astype(jnp.bfloat16)
     normed_two = rms_round(layer_one)

time: 211 us -> 199 us (0.943)
  between operations: 13.7 us -> 0.33 us
  waiting for transfers between devices: 87.1 us -> 79.9 us
  starting transfers between devices: 39 us -> 44.3 us
  local copies, waits for them, and re-layouts: 39.5 us -> 41.7 us
    all_gather x1 -> x0, waiting for transfers between devices: 27.9 us -> none  [on_device(): pooled_all = lax.all_gather(pooled, 'narrow', axis=1, tiled=True)]
    all_to_all x0 -> x1, waiting for transfers between devices: none -> 20.7 us  [on_device(): all_to_all(jnp.stack([pooled] * psum(1, 'narrow'), 0), 'narrow', 0, 0)]
    all_to_all x0 -> x1, starting transfers between devices: none -> 10.9 us  [on_device(): all_to_all(jnp.stack([pooled] * psum(1, 'narrow'), 0), 'narrow', 0, 0)]
    all_to_all x1, starting transfers between devices: 15 us -> 10.5 us  [on_device(): lax.all_to_all(packed(qkv_blocks, 0), 'wide', split_axis=0, concat_axis=0...]
  transfers between devices with their start and end apart: 5 -> 5, of which waited for: 4 -> 4; matrix products, arithmetic and copies ran while one was open for 14% -> 17% of each run, Pallas kernels for 0% -> 0%
where the time goes in v1:
time: 199 us; the launch traced here: 198 us
  waiting for transfers between devices  79.9 us (40%)
  starting transfers between devices  44.3 us (22%)
  local copies, waits for them, and re-layouts  41.7 us (21%)
  matrix products  23 us (12%)
  other arithmetic  7.28 us (4%)
    all_to_all x1, waiting for transfers between devices, on_device(): lax.all_to_all(packed(qkv_blocks, 0), 'wide', split_axis=0, concat_axis=0...  37.7 us
    all_to_all x1, waiting for transfers between devices, on_device(): all_to_all(jnp.stack([pooled] * psum(1, 'narrow'), 0), 'narrow', 0, 0)  20.7 us
    all_to_all x1, waiting for transfers between devices, on_device(): lax.all_to_all(mixture.reshape(wide_count, capacity, BLK, model_width), '...  17.3 us
    slice x11, local copies, waits for them, and re-layouts, split_heads(): block_rows[..., offset:offset + model_width]  12.7 us
    all_to_all x1, starting transfers between devices, on_device(): all_to_all(jnp.stack([pooled] * psum(1, 'narrow'), 0), 'narrow', 0, 0)  10.9 us
    all_to_all x1, starting transfers between devices, on_device(): lax.all_to_all(ball_packed, 'wide', split_axis=0, concat_axis=0, tiled=True)  10.6 us
    all_to_all x1, starting transfers between devices, on_device(): lax.all_to_all(packed(qkv_blocks, 0), 'wide', split_axis=0, concat_axis=0...  10.5 us
    scatter x3, local copies, waits for them, and re-layouts, packed(): return buffer.at[slot_of].set(block_data).reshape((wide_count, capacity)...  9.62 us
  transfers between devices with their start and end apart: 5, of which 4 were waited for; matrix products, arithmetic and copies ran while one was open for 17% of the time, Pallas kernels for 0%

profile of v1, /device:TPU:1, one launch (start us, length us, event | category | flops | bytes accessed | tf_op | source)
XLA Modules:
  0.0 197.8 jit_solution(924362978525560788)
XLA Ops:
  2.9 1.6 convolution_convert_fusion.1
  5.6 1.5 reshape.251
  7.1 1.4 reduce_sum.66
  10.6 10.9 %all-to-all-start = ((bf16[8,2,32,1024]{3,2,1,0:T(8,128)(2,1)}), bf16[8,2,32,1024]{3,2,1,0:T(8,128)(2,1)S(1)}, u32[]{:S(2)}, u32[]{:S(2)}) async-start(bf16[8,2,32,1024]{3,2,1,0:T(8,128)(2,1)} %stack.2), calls=%async_computation | async-start | bytes 2097152 | tf_op jit(solution)/shard_map/all_to_all | solution.py:120
  24.7 1.8 copy.52
  30.0 20.7 %all-to-all-done = bf16[8,2,32,1024]{3,2,1,0:T(8,128)(2,1)S(1)} async-done(((bf16[8,2,32,1024]{3,2,1,0:T(8,128)(2,1)}), bf16[8,2,32,1024]{3,2,1,0:T(8,128)(2,1)S(1)}, u32[]{:S(2)}, u32[]{:S(2)}) %all-to-all-start) | async-done | bytes 1048608 | tf_op jit(solution)/shard_map/all_to_all | solution.py:120
  50.7 10.6 %all-to-all-start.1 = ((s32[64,1,2]{2,1,0:T(1,128)}), s32[64,1,2]{2,1,0:T(1,128)S(1)}, u32[]{:S(2)}, u32[]{:S(2)}) async-start(s32[64,1,2]{2,1,0:T(1,128)} %bitcast.14), calls=%async_computation.1 | async-start | bytes 65536 | tf_op jit(solution)/shard_map/all_to_all | solution.py:152
  62.3 2.1 %copy.56 = bf16[2,256,512]{1,2,0:T(8,128)(2,1)} copy(bf16[2,256,512]{2,1,0:T(8,128)(2,1)} %get-tuple-element.129) | data formatting | bytes 1048576 | tf_op jit(solution)/shard_map/vmap()/slice | solution.py:28
  64.5 1.6 multiply_reduce_fusion
  74.1 1.6 broadcast_in_dim.71
  75.7 8.1 %scatter_fusion = bf16[128,4,1536]{2,1,0:T(4,128)(2,1)} fusion(bf16[128,4,1536]{2,1,0:T(4,128)(2,1)} %broadcast_in_dim.71, s32[64]{0:T(128)S(1)} %fusion.44, bf16[64,4,1536]{2,1,0:T(4,128)(2,1)S(1)} %reshape.294), kind=kCustom, calls=%fused_computation.3 | custom fusion | bytes 2359552 | tf_op jit(solution)/shard_map/scatter | solution.py:142
  83.8 10.5 %all-to-all-start.3 = ((bf16[64,2,4,1536]{3,2,1,0:T(4,128)(2,1)}), bf16[64,2,4,1536]{3,2,1,0:T(4,128)(2,1)S(1)}, u32[]{:S(2)}, u32[]{:S(2)}) async-start(bf16[64,2,4,1536]{3,2,1,0:T(4,128)(2,1)} %bitcast.17), calls=%async_computation.3 | async-start | bytes 3145728 | tf_op jit(solution)/shard_map/all_to_all | solution.py:151
  96.3 37.7 %all-to-all-done.3 = bf16[64,2,4,1536]{3,2,1,0:T(4,128)(2,1)S(1)} async-done(((bf16[64,2,4,1536]{3,2,1,0:T(4,128)(2,1)}), bf16[64,2,4,1536]{3,2,1,0:T(4,128)(2,1)S(1)}, u32[]{:S(2)}, u32[]{:S(2)}) %all-to-all-start.3) | async-done | bytes 1572896 | tf_op jit(solution)/shard_map/all_to_all | solution.py:151
  134.0 6.1 %all-to-all-start.2 = ((s32[64,1,2]{2,1,0:T(1,128)}), s32[64,1,2]{2,1,0:T(1,128)S(1)}, u32[]{:S(2)}, u32[]{:S(2)}) async-start(s32[64,1,2]{2,1,0:T(1,128)} %bitcast.21), calls=%async_computation.2 | async-start | bytes 65536 | tf_op jit(solution)/shard_map/all_to_all | solution.py:153
  141.5 1.5 fusion.56
  145.2 4.1 %all-to-all-done.2 = s32[64,1,2]{2,1,0:T(1,128)S(1)} async-done(((s32[64,1,2]{2,1,0:T(1,128)}), s32[64,1,2]{2,1,0:T(1,128)S(1)}, u32[]{:S(2)}, u32[]{:S(2)}) %all-to-all-start.2) | async-done | bytes 544 | tf_op jit(solution)/shard_map/all_to_all | solution.py:153
  149.4 20.9 %while.11 = (s32[]{:T(128)}, bf16[2,256,512]{2,1,0:T(8,128)(2,1)}, s32[2]{0:T(128)S(1)}, s32[512]{0:T(512)S(1)}, bf16[512,8,64]{0,2,1:T(8,128)(2,1)S(1)}, /*inde...) while((s32[]{:T(128)}, bf16[2,256,512]{2,1,0:T(8,128)(2,1)}, ...), condition=%wide.region_15.16_spmd.clone, body=%wide.region_12.15_spmd.clone.sunk | while | flops 275121152 | bytes 11303615 | solution.py:107
  151.4 4.5 %fusion.79 = (f32[8,256]{1,0:T(8,128)S(1)}, f32[8,256,512]{2,1,0:T(8,128)}) fusion(pred[256,512]{1,0:T(8,128)(4,1)S(1)} %compare_and_fusion.2, bf16[512,8,64]{0,2,1:T(8,128)(2,1)} %get-tuple-element.229, bf16[512,8,64]{0,2,1:T(8,128)(2,1)S(1)} %get-tuple-element.228, s32[]{:T(128)S(6)} %select_n.46), kind=kOutput, calls=%fused_computation.77.clone.1 | convolution fusion | flops 138412544 | bytes 5120004 | tf_op jit(solution)/shard_map/while/body/eval_jaxpr/sub | solution.py:100
  155.9 3.0 %fusion.80 = bf16[8,256,64]{1,2,0:T(8,128)(2,1)S(1)} fusion(bf16[512,8,64]{0,2,1:T(8,128)(2,1)S(1)} %get-tuple-element.230, f32[8,256,512]{2,1,0:T(8,128)} %get-tuple-element.196, f32[8,256]{1,0:T(8,128)S(1)} %get-tuple-element.197), kind=kOutput, calls=%fused_computation.15.clone.1 | convolution fusion | flops 136445952 | bytes 4988928 | tf_op jit(solution)/shard_map/while/body/eval_jaxpr/hqk,khe->qhe/dot_general | solution.py:102
  161.9 4.5 %fusion.79 = (f32[8,256]{1,0:T(8,128)S(1)}, f32[8,256,512]{2,1,0:T(8,128)}) fusion(pred[256,512]{1,0:T(8,128)(4,1)S(1)} %compare_and_fusion.2, bf16[512,8,64]{0,2,1:T(8,128)(2,1)} %get-tuple-element.229, bf16[512,8,64]{0,2,1:T(8,128)(2,1)S(1)} %get-tuple-element.228, s32[]{:T(128)S(6)} %select_n.46), kind=kOutput, calls=%fused_computation.77.clone.1 | convolution fusion | flops 138412544 | bytes 5120004 | tf_op jit(solution)/shard_map/while/body/eval_jaxpr/sub | solution.py:100
  166.4 3.0 %fusion.80 = bf16[8,256,64]{1,2,0:T(8,128)(2,1)S(1)} fusion(bf16[512,8,64]{0,2,1:T(8,128)(2,1)S(1)} %get-tuple-element.230, f32[8,256,512]{2,1,0:T(8,128)} %get-tuple-element.196, f32[8,256]{1,0:T(8,128)S(1)} %get-tuple-element.197), kind=kOutput, calls=%fused_computation.15.clone.1 | convolution fusion | flops 136445952 | bytes 4988928 | tf_op jit(solution)/shard_map/while/body/eval_jaxpr/hqk,khe->qhe/dot_general | solution.py:102
  170.3 2.1 %reshape_reshape.4 = bf16[64,2,4,512]{3,2,1,0:T(4,128)(2,1)} reshape(bf16[2,256,512]{2,1,0:T(8,128)(2,1)} %get-tuple-element.52) | data formatting | bytes 1048576 | tf_op jit(solution)/shard_map/reshape;reshape | solution.py:160
  172.4 6.2 %all-to-all-start.4 = ((bf16[64,2,4,512]{3,2,1,0:T(4,128)(2,1)}), bf16[64,2,4,512]{3,2,1,0:T(4,128)(2,1)S(1)}, u32[]{:S(2)}, u32[]{:S(2)}) async-start(bf16[64,2,4,512]{3,2,1,0:T(4,128)(2,1)} %reshape_reshape.4), calls=%async_computation.4 | async-start | bytes 1048576 | tf_op jit(solution)/shard_map/all_to_all | solution.py:159
  178.6 17.3 %all-to-all-done.4 = bf16[64,2,4,512]{3,2,1,0:T(4,128)(2,1)S(1)} async-done(((bf16[64,2,4,512]{3,2,1,0:T(4,128)(2,1)}), bf16[64,2,4,512]{3,2,1,0:T(4,128)(2,1)S(1)}, u32[]{:S(2)}, u32[]{:S(2)}) %all-to-all-start.4) | async-done | bytes 524320 | tf_op jit(solution)/shard_map/all_to_all | solution.py:159
  (106 shorter events, 33.7 us)
Async XLA Ops:
  0.0 2.9 %copy-start = (bf16[512,1536]{1,0:T(8,128)(2,1)S(1)}, bf16[512,1536]{1,0:T(8,128)(2,1)}, u32[]{:S(2)}) copy-start(bf16[512,1536]{1,0:T(8,128)(2,1)} %param.14) | copy-start | bytes 4718596
  10.6 40.1 %all-to-all-start = ((bf16[8,2,32,1024]{3,2,1,0:T(8,128)(2,1)}), bf16[8,2,32,1024]{3,2,1,0:T(8,128)(2,1)S(1)}, u32[]{:S(2)}, u32[]{:S(2)}) async-start(bf16[8,2,32,1024]{3,2,1,0:T(8,128)(2,1)} %stack.2), calls=%async_computation | async-start | bytes 2097152 | tf_op jit(solution)/shard_map/all_to_all | solution.py:120
  21.5 5.0 %copy-start.14 = (s32[2,32]{1,0:T(2,128)S(1)}, s32[2,32]{1,0:T(2,128)}, u32[]{:S(2)}) copy-start(s32[2,32]{1,0:T(2,128)} %param.12) | copy-start | bytes 772
  21.5 5.1 %copy-start.15 = (s32[2,32]{1,0:T(2,128)S(1)}, s32[2,32]{1,0:T(2,128)}, u32[]{:S(2)}) copy-start(s32[2,32]{1,0:T(2,128)} %param.13) | copy-start | bytes 772
  50.7 33.1 %all-to-all-start.1 = ((s32[64,1,2]{2,1,0:T(1,128)}), s32[64,1,2]{2,1,0:T(1,128)S(1)}, u32[]{:S(2)}, u32[]{:S(2)}) async-start(s32[64,1,2]{2,1,0:T(1,128)} %bitcast.14), calls=%async_computation.1 | async-start | bytes 65536 | tf_op jit(solution)/shard_map/all_to_all | solution.py:152
  62.3 3.8 %copy-start.5 = (f32[2,8,128,128]{2,3,1,0:T(8,128)S(1)}, f32[2,8,128,128]{2,3,1,0:T(8,128)}, u32[]{:S(2)}) copy-start(f32[2,8,128,128]{2,3,1,0:T(8,128)} %get-tuple-element.134) | copy-start | bytes 3145732
  66.1 1.4 copy-start.1
  66.1 3.1 %copy-start.12 = (bf16[2,128,512]{1,2,0:T(8,128)(2,1)S(1)}, bf16[2,128,512]{1,2,0:T(8,128)(2,1)}, u32[]{:S(2)}) copy-start(bf16[2,128,512]{1,2,0:T(8,128)(2,1)} %copy.52) | copy-start | bytes 786436
  69.2 1.6 copy-start.2
  69.2 1.7 copy-start.10
  70.8 1.1 copy-start.6
  70.8 1.1 copy-start.11
  71.9 1.4 copy-start.7
  72.4 0.8 copy-start.3
  83.8 10.5 %copy-start.13 = (s32[2,32]{1,0:T(2,128)S(1)}, s32[2,32]{1,0:T(2,128)}, u32[]{:S(2)}) copy-start(s32[2,32]{1,0:T(2,128)} %param.11) | copy-start | bytes 772
  83.8 50.3 %all-to-all-start.3 = ((bf16[64,2,4,1536]{3,2,1,0:T(4,128)(2,1)}), bf16[64,2,4,1536]{3,2,1,0:T(4,128)(2,1)S(1)}, u32[]{:S(2)}, u32[]{:S(2)}) async-start(bf16[64,2,4,1536]{3,2,1,0:T(4,128)(2,1)} %bitcast.17), calls=%async_computation.3 | async-start | bytes 3145728 | tf_op jit(solution)/shard_map/all_to_all | solution.py:151
  134.0 15.3 %all-to-all-start.2 = ((s32[64,1,2]{2,1,0:T(1,128)}), s32[64,1,2]{2,1,0:T(1,128)S(1)}, u32[]{:S(2)}, u32[]{:S(2)}) async-start(s32[64,1,2]{2,1,0:T(1,128)} %bitcast.21), calls=%async_computation.2 | async-start | bytes 65536 | tf_op jit(solution)/shard_map/all_to_all | solution.py:153
  144.0 5.4 %copy-start.9 = (bf16[512,512]{0,1:T(8,128)(2,1)S(1)}, bf16[512,512]{0,1:T(8,128)(2,1)}, u32[]{:S(2)}) copy-start(bf16[512,512]{0,1:T(8,128)(2,1)} %copy.63) | copy-start | bytes 1572868
  170.3 26.5 %copy-start.4 = (f32[2,128,512]{2,1,0:T(8,128)S(1)}, f32[2,128,512]{2,1,0:T(8,128)}, u32[]{:S(2)}) copy-start(f32[2,128,512]{2,1,0:T(8,128)} %copy-done.3) | copy-start | bytes 1572868
  170.3 26.5 %copy-start.8 = (bf16[512,512]{1,0:T(8,128)(2,1)S(1)}, bf16[512,512]{1,0:T(8,128)(2,1)}, u32[]{:S(2)}) copy-start(bf16[512,512]{1,0:T(8,128)(2,1)} %param.17) | copy-start | bytes 1572868
  172.4 23.5 %all-to-all-start.4 = ((bf16[64,2,4,512]{3,2,1,0:T(4,128)(2,1)}), bf16[64,2,4,512]{3,2,1,0:T(4,128)(2,1)S(1)}, u32[]{:S(2)}, u32[]{:S(2)}) async-start(bf16[64,2,4,512]{3,2,1,0:T(4,128)(2,1)} %reshape_reshape.4), calls=%async_computation.4 | async-start | bytes 1048576 | tf_op jit(solution)/shard_map/all_to_all | solution.py:159
